TPU v7x, 128 devices: a whole 4x4x4 slice. The times are simulated.
128 devices in a mesh: row: 16 (over x, z), col: 8 (over y, core).
Axes of the slice: x: 4, y: 4, z: 4, core: 2. Of those that a mesh axis runs over, the one named last changes fastest.
Arguments:
- amplitudes: bfloat16 [16384, 16384], P('row', 'col'), may hold values from -6 to 6
- integrals: bfloat16 [16384, 4096], P('col', 'row'), may hold values from -0.046875 to 0.046875
- amp_mask: int32 [128, 128], P('row', 'col'), may hold values 0 or 1
- int_mask: int32 [128, 32], P('col', 'row'), may hold values 0 or 1
Outputs:
- ladder: bfloat16 [16384, 4096], P('row', 'col')
All inputs are finite; a program needn't handle non-finite values. No bound on the sum of `amp_mask` or of `int_mask` on one device may be relied on, other than what follows from the above.
Results may differ from a plain program's by a relative error of at most 0.001.
Values may be sent and summed in bfloat16 or wider, within the bound.
A program may use at most 128 MiB of HBM per device.

v0:
```python
import jax
import jax.numpy as jnp
from jax import lax
from jax.sharding import PartitionSpec as P

TILE = 128


def expand(mask):
    spread = jnp.repeat(jnp.repeat(mask, TILE, axis=0), TILE, axis=1)
    return spread.astype(jnp.bfloat16)


def per_device(amplitudes, integrals, amp_mask, int_mask):
    sparse_amp = amplitudes * expand(amp_mask)
    sparse_int = integrals * expand(int_mask)
    partial_value = jnp.dot(
        sparse_amp,
        lax.all_gather(sparse_int, "row", axis=1, tiled=True),
        preferred_element_type=jnp.float32,
    )
    ladder = lax.psum_scatter(partial_value, "col", scatter_dimension=1, tiled=True)
    return ladder.astype(jnp.bfloat16)


def solution(mesh):
    in_specs = (P("row", "col"), P("col", "row"), P("row", "col"), P("col", "row"))
    out_specs = P("row", "col")
    return jax.shard_map(
        per_device, mesh=mesh, in_specs=in_specs, out_specs=out_specs, check_vma=False
    )
```

profile of v0, /device:TPU:5, one launch (start us, length us, event | category | flops | bytes accessed | tf_op | source)
XLA Modules:
  0.0 265.0 jit_solution(4168106295409174461)
XLA Ops:
  6.5 0.0 copy-start
  6.5 0.0 all-gather.2.cloned.1.call-start
  6.5 0.7 convert_element_type.28
  7.2 0.1 copy.5
  7.3 0.1 broadcast_in_dim.14
  7.4 5.8 %broadcast_in_dim.15 = bf16[2048,2,128]{2,1,0:T(2,128)(2,1)S(1)} broadcast(bf16[2048,2]{1,0:T(8,128)(2,1)S(1)} %bitcast.12), dimensions={0,1} | broadcast | bytes 1056768 | tf_op jit(solution)/shard_map/broadcast_in_dim | solution.py:10
  13.2 2.4 bitcast_multiply_fusion.2
  15.6 0.0 all-gather.2.cloned.1.call-update
  15.6 0.0 reduce-scatter.2.cloned.1.call-start
  15.6 0.0 copy-done
  15.7 119.5 %all-gather.2.cloned.1.call-done = bf16[2048,4096]{1,0:T(8,128)(2,1)} async-done(((bf16[2048,256]{1,0:T(8,128)(2,1)}), bf16[2048,4096]{1,0:T(8,128)(2,1)}) %all-gather.2.cloned.1.call-update) | async-done | bytes 16777232 | tf_op jit(solution)/shard_map/all_gather | solution.py:19
  135.2 0.0 copy-start.1
  135.2 4.5 %broadcast_in_dim.13 = bf16[1024,16,128]{2,1,0:T(8,128)(2,1)S(1)} broadcast(bf16[1024,16]{1,0:T(8,128)(2,1)S(1)} %bitcast.13), dimensions={0,1} | broadcast | bytes 4227072 | tf_op jit(solution)/shard_map/broadcast_in_dim | solution.py:10
  139.7 0.0 copy-done.1
  139.7 22.2 %fusion = f32[1024,4096]{1,0:T(8,128)} fusion(bf16[2048,4096]{1,0:T(8,128)(2,1)} %all-gather.2.cloned.1.call-done, bf16[1024,2048]{1,0:T(8,128)(2,1)S(1)} %copy-done.1, bf16[128,8,16,128]{3,2,1,0:T(8,128)(2,1)S(1)} %bitcast.11), kind=kOutput, calls=%fused_computation.1 | convolution fusion | flops 17181966336 | bytes 41943040 | tf_op jit(solution)/shard_map/dot_general | solution.py:17
  161.9 0.0 reduce-scatter.2.cloned.1.call-update
  162.0 93.5 %reduce-scatter.2.cloned.1.call-done = f32[1024,512]{1,0:T(8,128)} async-done(((f32[1024,4096]{1,0:T(8,128)}), f32[1024,512]{1,0:T(8,128)}) %reduce-scatter.2.cloned.1.call-update) | async-done | bytes 2097168 | tf_op jit(solution)/shard_map/reduce_scatter | solution.py:22
  255.5 2.7 %convert_element_type.31 = bf16[1024,512]{1,0:T(8,128)(2,1)} convert(f32[1024,512]{1,0:T(8,128)} %reduce-scatter.2.cloned.1.call-done) | non-fusion elementwise | flops 524288 | bytes 3145728 | tf_op jit(solution)/shard_map/convert_element_type | solution.py:23
  (2 shorter events, 0.0 us)
Async XLA Ops:
  6.5 9.1 %copy-start = (s32[8,16]{1,0:T(8,128)S(1)}, s32[8,16]{1,0:T(8,128)}, u32[]{:S(2)}) copy-start(s32[8,16]{1,0:T(8,128)} %param.6) | copy-start | bytes 1540
  6.5 128.6 %all-gather.2.cloned.1.call-start = ((), (), s32[]{:S(2)}) async-start(), calls=%async_computation.1 | async-start | bytes 17825792 | tf_op jit(solution)/shard_map/all_gather | solution.py:19
  15.6 239.9 %reduce-scatter.2.cloned.1.call-start = ((), (), s32[]{:S(2)}) async-start(), calls=%async_computation.2 | async-start | bytes 18874368 | tf_op jit(solution)/shard_map/reduce_scatter | solution.py:22
  135.2 4.5 %copy-start.1 = (bf16[1024,2048]{1,0:T(8,128)(2,1)S(1)}, bf16[1024,2048]{1,0:T(8,128)(2,1)}, u32[]{:S(2)}) copy-start(bf16[1024,2048]{1,0:T(8,128)(2,1)} %param.4) | copy-start | bytes 12582916
Sparse Core Ops, SparseCore 0:
  15.7 119.4 all-gather.1
  162.1 93.3 reduce-scatter.1
where the time goes:
time: 266 us; the launch traced here: 265 us
  waiting for transfers between devices  213 us (80%)
  matrix products  22.2 us (8%)
  between operations  13.4 us (5%)
  local copies, waits for them, and re-layouts  10.5 us (4%)
  other arithmetic  5.77 us (2%)
    all_gather x1, waiting for transfers between devices, per_device(): lax.all_gather(sparse_int, 'row', axis=1, tiled=True)  120 us
    reduce_scatter x1, waiting for transfers between devices, per_device(): lax.psum_scatter(partial_value, 'col', scatter_dimension=1, tiled=True)  93.5 us
    dot_general x1, matrix products, per_device(): jnp.dot(sparse_amp, lax.all_gather(sparse_int, 'row', axis=1, tiled=True)...  22.2 us
    broadcast_in_dim x4, local copies, waits for them, and re-layouts, expand(): spread = jnp.repeat(jnp.repeat(mask, TILE, axis=0), TILE, axis=1)  10.4 us
  transfers between devices with their start and end apart: 2, of which 2 were waited for; matrix products, arithmetic and copies ran while one was open for 0% of the time, Pallas kernels for 0%

commit v1 on v0

v1 whole, which is shorter than its diff:
```python
import jax
import jax.numpy as jnp
from jax import lax
from jax.experimental import pallas as pl
from jax.experimental.pallas import tpu as pltpu
from jax.sharding import PartitionSpec as P

MESH = pl.DeviceIdType.MESH
TILE = 128
ROWS = 1024
DEPTH = 2048
WIDE = 128
BLOCK = 256
STEP = (0, 3, 1, 2)


def kernel(
    a_hbm, b_hbm, am, im, o_hbm,
    a_buf, b_raw, b_out, b_buf, c_buf, near, mine, out_buf, out_send,
    load_sem, pair_s, pair_r, ring_s, ring_r, y_s, y_r, o_s, o_r, store_sem,
):
    r, q = lax.axis_index("row"), lax.axis_index("col")
    x, z, y, c = r // 4, r % 4, q // 2, q % 2

    def dev(x_, z_, y_, c_):
        return (x_ * 4 + z_, y_ * 2 + c_)

    sibling = dev(x, z, y, 1 - c)
    on_x, on_z = 1 - c, c

    def along_first(d):
        return dev((x + d * on_x) % 4, (z + d * on_z) % 4, y, c)

    def along_second(d):
        return dev((x + d * on_z) % 4, (z + d * on_x) % 4, y, c)

    def along_y(d):
        return dev(x, z, (y + d) % 4, c)

    started = []

    def send(src, dst, ss, rs, to):
        copy = pltpu.make_async_remote_copy(
            src_ref=src, dst_ref=dst, send_sem=ss, recv_sem=rs, device_id=to, device_id_type=MESH
        )
        copy.start()
        return copy

    def arrived(dst, rs):
        pltpu.make_async_remote_copy(
            src_ref=dst, dst_ref=dst, send_sem=rs, recv_sem=rs, device_id=sibling, device_id_type=MESH
        ).wait_recv()

    loads = [
        pltpu.make_async_copy(b_hbm.at[:, pl.ds(h * WIDE, WIDE)], b_raw.at[h], load_sem.at[h])
        for h in range(2)
    ] + [pltpu.make_async_copy(a_hbm, a_buf.at[c], load_sem.at[2])]
    for load in loads:
        load.start()

    barrier = pltpu.get_barrier_semaphore()
    peers = [sibling]
    for d in (1, 3):
        peers += [along_first(d), along_second(d), along_y(d)]
    for peer in peers:
        pl.semaphore_signal(barrier, inc=1, device_id=peer, device_id_type=MESH)

    loads[0].wait()
    loads[1].wait()

    def mask_b(t, carry):
        rows = pl.ds(pl.multiple_of(t * TILE, TILE), TILE)
        keep = im[t, 1 - c].astype(jnp.float32)
        b_out[rows, :] = (b_raw[1 - c, rows, :].astype(jnp.float32) * keep).astype(jnp.bfloat16)
        keep = im[t, c].astype(jnp.float32)
        b_buf[0, 0, c, rows, :] = (b_raw[c, rows, :].astype(jnp.float32) * keep).astype(jnp.bfloat16)
        return carry

    lax.fori_loop(0, DEPTH // TILE, mask_b, 0)
    pl.semaphore_wait(barrier, 7)

    def ring(i, j, h, ti, tj, direction, to):
        started.append(
            send(
                b_buf.at[i, j, h], b_buf.at[ti, tj, h],
                ring_s.at[i, j, h, direction], ring_r.at[ti, tj, h], to,
            )
        )

    def got(i, j, h):
        arrived(b_buf.at[i, j, h], ring_r.at[i, j, h])

    def first_out(h):
        ring(0, 0, h, 1, 0, 0, along_first(1))
        ring(0, 0, h, 2, 0, 1, along_first(3))

    def second_out(i, h):
        ring(i, 0, h, i, 1, 2, along_second(1))
        ring(i, 0, h, i, 2, 3, along_second(3))

    started.append(send(b_out, b_buf.at[0, 0, c], pair_s.at[0], pair_r.at[0], sibling))
    first_out(c)
    second_out(0, c)

    loads[2].wait()

    def mask_a(t, carry):
        rows = pl.ds(pl.multiple_of(t * TILE, TILE), TILE)
        for k in range(DEPTH // TILE):
            cols = pl.ds(k * TILE, TILE)
            keep = am[t, k].astype(jnp.float32)
            a_buf[c, rows, cols] = (a_buf[c, rows, cols].astype(jnp.float32) * keep).astype(jnp.bfloat16)
        return carry

    lax.fori_loop(0, ROWS // TILE, mask_a, 0)
    arrived(b_buf.at[0, 0, 1 - c], pair_r.at[0])
    first_out(1 - c)
    second_out(0, 1 - c)
    started.append(send(a_buf.at[c], a_buf.at[c], pair_s.at[1], pair_r.at[1], sibling))

    def first_forward():
        got(1, 0, 0)
        ring(1, 0, 0, 3, 0, 0, along_first(1))
        got(2, 0, 1)
        ring(2, 0, 1, 3, 0, 1, along_first(3))
        got(1, 0, 1)
        got(2, 0, 0)

    def second_forward(i):
        got(i, 1, 0)
        ring(i, 1, 0, i, 3, 2, along_second(1))
        got(i, 2, 1)
        ring(i, 2, 1, i, 3, 3, along_second(3))

    def second_rest(i):
        got(i, 1, 1)
        got(i, 2, 0)

    def product(*slots):
        def step(t, carry):
            rows = pl.ds(pl.multiple_of(t * BLOCK, BLOCK), BLOCK)
            total = None
            for h in range(2):
                units = [b_buf[i, j, h] for i, j in slots]
                unit = units[0] if len(units) == 1 else jnp.concatenate(units, axis=1)
                part = jnp.dot(a_buf[h, rows, :], unit, preferred_element_type=jnp.float32)
                total = part if total is None else total + part
            for n, (i, j) in enumerate(slots):
                c_buf[i * 4 + j, rows, :] = total[:, n * WIDE : (n + 1) * WIDE]
            return carry

        lax.fori_loop(0, ROWS // BLOCK, step, 0)

    def place(i, j):
        di, dj = STEP[i], STEP[j]
        return (x + di * on_x + dj * on_z) % 4, (z + di * on_z + dj * on_x) % 4

    HALF = ROWS // 2

    def half(n):
        return pl.ds(n * HALF, HALF)

    def y_copy(u, n, dst, ss, rs, to):
        return pltpu.make_async_remote_copy(
            src_ref=c_buf.at[u, half(n)], dst_ref=dst, send_sem=ss, recv_sem=rs, device_id=to, device_id_type=MESH
        )

    def far_copy(u, n, zz):
        return y_copy(u, n, near.at[n, zz], y_s.at[u, n], y_r.at[n, zz], along_y(3 if n == 0 else 1))

    def near_copy(u, n, side, zz):
        return y_copy(
            u, n, mine.at[side, zz, half(n)], y_s.at[u, n], y_r.at[2 + side * 2 + n, zz], along_y(3 if side == 0 else 1)
        )

    def pass_on(i, j):
        u = i * 4 + j
        xx, zz = place(i, j)
        role = (y - xx + 4) % 4

        @pl.when(role == 2)
        def _():
            far_copy(u, 0, zz).start()
            far_copy(u, 1, zz).start()

        @pl.when(role == 1)
        def _():
            near_copy(u, 1, 0, zz).start()

        @pl.when(role == 3)
        def _():
            near_copy(u, 0, 1, zz).start()

    def add_on(i, j):
        u = i * 4 + j
        xx, zz = place(i, j)
        role = (y - xx + 4) % 4

        def add(n, side):
            arrived(near.at[n, zz], y_r.at[n, zz])
            c_buf[u, half(n), :] = c_buf[u, half(n), :] + near[n, zz]
            near_copy(u, n, side, zz).start()

        @pl.when(role == 1)
        def _():
            add(0, 0)

        @pl.when(role == 3)
        def _():
            add(1, 1)

    waiting = []

    def run(*slots):
        product(*slots)
        for i, j in slots:
            pass_on(i, j)
        for i, j in waiting:
            add_on(i, j)
        waiting[:] = slots

    arrived(a_buf.at[1 - c], pair_r.at[1])
    run((0, 0))
    first_forward()
    for h in range(2):
        second_out(1, h)
    second_forward(0)
    for h in range(2):
        second_out(2, h)
    run((1, 0), (2, 0))
    second_rest(0)
    run((0, 1), (0, 2))
    got(3, 0, 0)
    got(3, 0, 1)
    for h in range(2):
        second_out(3, h)
    got(0, 3, 0)
    got(0, 3, 1)
    second_forward(1)
    run((3, 0), (0, 3))
    second_rest(1)
    run((1, 1), (1, 2))
    second_forward(2)
    second_rest(2)
    run((2, 1), (2, 2))
    second_forward(3)
    for i in (1, 2):
        got(i, 3, 0)
        got(i, 3, 1)
    run((1, 3), (2, 3))
    second_rest(3)
    run((3, 1), (3, 2))
    got(3, 3, 0)
    got(3, 3, 1)
    run((3, 3))
    for i, j in waiting:
        add_on(i, j)

    ahead = (y - x + 4) % 4
    slot = (ahead == 1) * 2 + (ahead == 2) * 3 + (ahead == 3) * 1

    def own(j):
        u = jnp.where(c == 0, slot * 4 + j, j * 4 + slot)
        zz = (z + STEP[j]) % 4
        return u, zz

    def store(n):
        return pltpu.make_async_copy(
            out_buf.at[n], o_hbm.at[:, pl.ds(n * WIDE, WIDE)], store_sem.at[n]
        )

    for j in range(4):
        u, zz = own(j)
        for side in range(2):
            for n in range(2):
                arrived(mine.at[side, zz, half(n)], y_r.at[2 + side * 2 + n, zz])
        spot = (zz % 2) * 2 + c
        stays = zz // 2 == c

        def value(t):
            rows = pl.ds(pl.multiple_of(t * TILE, TILE), TILE)
            return rows, (c_buf[u, rows, :] + (mine[0, zz, rows, :] + mine[1, zz, rows, :])).astype(jnp.bfloat16)

        @pl.when(stays)
        def _():
            def step(t, carry):
                rows, v = value(t)
                out_buf[spot, rows, :] = v
                return carry

            lax.fori_loop(0, ROWS // TILE, step, 0)

        @pl.when(jnp.logical_not(stays))
        def _():
            def step(t, carry):
                rows, v = value(t)
                out_send[zz % 2, rows, :] = v
                return carry

            lax.fori_loop(0, ROWS // TILE, step, 0)
            send(out_send.at[zz % 2], out_buf.at[spot], o_s.at[zz % 2], o_r.at[zz % 2], sibling)

    for n in range(2):
        arrived(out_buf.at[n * 2 + 1 - c], o_r.at[n])
    for n in range(4):
        store(n).start()

    for copy in started:
        copy.wait_send()
    for u in range(16):
        i, j = u // 4, u % 4
        xx, zz = place(i, j)
        role = (y - xx + 4) % 4

        @pl.when(role != 0)
        def _():
            for n in range(2):
                far_copy(u, n, zz).wait_send()

    for n in range(2):
        pltpu.make_async_remote_copy(
            src_ref=out_send.at[n], dst_ref=out_send.at[n], send_sem=o_s.at[n], recv_sem=o_s.at[n],
            device_id=sibling, device_id_type=MESH,
        ).wait_send()
    for n in range(4):
        store(n).wait()


def per_device(amplitudes, integrals, amp_mask, int_mask):
    bf16, f32 = jnp.bfloat16, jnp.float32
    dma = pltpu.SemaphoreType.DMA
    return pl.pallas_call(
        kernel,
        out_shape=jax.ShapeDtypeStruct((ROWS, 4 * WIDE), bf16),
        in_specs=[
            pl.BlockSpec(memory_space=pl.ANY),
            pl.BlockSpec(memory_space=pl.ANY),
            pl.BlockSpec(memory_space=pltpu.SMEM),
            pl.BlockSpec(memory_space=pltpu.SMEM),
        ],
        out_specs=pl.BlockSpec(memory_space=pl.ANY),
        scratch_shapes=[
            pltpu.VMEM((2, ROWS, DEPTH), bf16),
            pltpu.VMEM((2, DEPTH, WIDE), bf16),
            pltpu.VMEM((DEPTH, WIDE), bf16),
            pltpu.VMEM((4, 4, 2, DEPTH, WIDE), bf16),
            pltpu.VMEM((16, ROWS, WIDE), f32),
            pltpu.VMEM((2, 4, ROWS // 2, WIDE), f32),
            pltpu.VMEM((2, 4, ROWS, WIDE), f32),
            pltpu.VMEM((4, ROWS, WIDE), bf16),
            pltpu.VMEM((2, ROWS, WIDE), bf16),
            dma((3,)),
            dma((2,)),
            dma((2,)),
            dma((4, 4, 2, 4)),
            dma((4, 4, 2)),
            dma((16, 2)),
            dma((6, 4)),
            dma((2,)),
            dma((2,)),
            dma((4,)),
        ],
        compiler_params=pltpu.CompilerParams(
            collective_id=0, has_side_effects=True, vmem_limit_bytes=60 << 20
        ),
    )(amplitudes, integrals, amp_mask, int_mask)


def solution(mesh):
    in_specs = (P("row", "col"), P("col", "row"), P("row", "col"), P("col", "row"))
    out_specs = P("row", "col")
    return jax.shard_map(
        per_device, mesh=mesh, in_specs=in_specs, out_specs=out_specs, check_vma=False
    )
```

time: 266 us -> 144 us (0.54)
  waiting for transfers between devices: 213 us -> 0 us
  Pallas kernels: 0 us -> 140 us
  matrix products: 22.2 us -> 0 us
  between operations: 13.4 us -> 0.01 us
  local copies, waits for them, and re-layouts: 10.5 us -> 3.61 us
  other arithmetic: 5.77 us -> 0 us
    pallas_call x0 -> x1, Pallas kernels: none -> 140 us  [per_device(): pl.pallas_call(kernel, out_shape=jax.ShapeDtypeStruct((ROWS, 4 * WIDE), b...]
    all_gather x1 -> x0, waiting for transfers between devices: 120 us -> none  [per_device(): lax.all_gather(sparse_int, 'row', axis=1, tiled=True)]
    reduce_scatter x1 -> x0, waiting for transfers between devices: 93.5 us -> none  [per_device(): lax.psum_scatter(partial_value, 'col', scatter_dimension=1, tiled=True)]
    dot_general x1 -> x0, matrix products: 22.2 us -> none  [per_device(): jnp.dot(sparse_amp, lax.all_gather(sparse_int, 'row', axis=1, tiled=True)...]
    broadcast_in_dim x4 -> x0, local copies, waits for them, and re-layouts: 10.4 us -> none  [expand(): spread = jnp.repeat(jnp.repeat(mask, TILE, axis=0), TILE, axis=1)]
    unnamed x4 -> x2, local copies, waits for them, and re-layouts: 0.01 us -> 3.61 us
    convert_element_type x3 -> x0, other arithmetic: 3.39 us -> none  [the longest x1 2.69 us: per_device(): return ladder.astype(jnp.bfloat16)]
  transfers between devices with their start and end apart: 2 -> 0, of which waited for: 2 -> 0; matrix products, arithmetic and copies ran while one was open for 0% -> 0% of each run, Pallas kernels for 0% -> 0%
where the time goes in v1:
time: 144 us
  Pallas kernels  140 us (97%)
  local copies, waits for them, and re-layouts  3.61 us (3%)
    pallas_call x1, Pallas kernels, per_device(): pl.pallas_call(kernel, out_shape=jax.ShapeDtypeStruct((ROWS, 4 * WIDE), b...  140 us
    unnamed x2, local copies, waits for them, and re-layouts  3.61 us

profile of v1, /device:TPU:5, one launch (start us, length us, event | category | flops | bytes accessed | tf_op | source)
XLA Modules:
  0.0 143.8 jit_solution(17082460949495109101)
XLA Ops:
  0.0 1.4 copy.5.im
  1.4 140.2 %shard_map.46 = bf16[1024,512]{1,0:T(8,128)(2,1)} custom-call(bf16[1024,2048]{1,0:T(8,128)(2,1)} %a_hbm.1, bf16[2048,256]{1,0:T(8,128)(2,1)} %b_hbm.1, s32[8,16]{1,0:T(8,128)} %am.1, s32[16,2]{1,0:T(8,128)} %copy.5.im), custom_call_target="tpu_custom_call" | custom-call | tf_op jit(solution)/shard_map/pallas_call | solution.py:332
  141.5 2.3 %copy.7 = bf16[1024,512]{1,0:T(8,128)(2,1)} copy(bf16[1024,512]{1,0:T(8,128)(2,1)} %shard_map.46) | data formatting | bytes 2097152

commit v2 on v1

--- a/solution.py
+++ b/solution.py
@@ -70,9 +70,9 @@
 
     def mask_b(t, carry):
         rows = pl.ds(pl.multiple_of(t * TILE, TILE), TILE)
-        keep = im[t, 1 - c].astype(jnp.float32)
+        keep = im[1 - c, t].astype(jnp.float32)
         b_out[rows, :] = (b_raw[1 - c, rows, :].astype(jnp.float32) * keep).astype(jnp.bfloat16)
-        keep = im[t, c].astype(jnp.float32)
+        keep = im[c, t].astype(jnp.float32)
         b_buf[0, 0, c, rows, :] = (b_raw[c, rows, :].astype(jnp.float32) * keep).astype(jnp.bfloat16)
         return carry
 
@@ -94,13 +94,8 @@
         ring(0, 0, h, 1, 0, 0, along_first(1))
         ring(0, 0, h, 2, 0, 1, along_first(3))
 
-    def second_out(i, h):
-        ring(i, 0, h, i, 1, 2, along_second(1))
-        ring(i, 0, h, i, 2, 3, along_second(3))
-
     started.append(send(b_out, b_buf.at[0, 0, c], pair_s.at[0], pair_r.at[0], sibling))
     first_out(c)
-    second_out(0, c)
 
     loads[2].wait()
 
@@ -115,26 +110,25 @@
     lax.fori_loop(0, ROWS // TILE, mask_a, 0)
     arrived(b_buf.at[0, 0, 1 - c], pair_r.at[0])
     first_out(1 - c)
-    second_out(0, 1 - c)
     started.append(send(a_buf.at[c], a_buf.at[c], pair_s.at[1], pair_r.at[1], sibling))
 
-    def first_forward():
-        got(1, 0, 0)
-        ring(1, 0, 0, 3, 0, 0, along_first(1))
-        got(2, 0, 1)
-        ring(2, 0, 1, 3, 0, 1, along_first(3))
-        got(1, 0, 1)
-        got(2, 0, 0)
-
-    def second_forward(i):
-        got(i, 1, 0)
-        ring(i, 1, 0, i, 3, 2, along_second(1))
-        got(i, 2, 1)
-        ring(i, 2, 1, i, 3, 3, along_second(3))
+    def first_forward(h):
+        got(1 + h, 0, h)
+        ring(1 + h, 0, h, 3, 0, h, along_first(1 + 2 * h))
+
+    def second_forward(i, h):
+        got(i, 1 + h, h)
+        ring(i, 1 + h, h, i, 3, 2 + h, along_second(1 + 2 * h))
 
     def second_rest(i):
         got(i, 1, 1)
         got(i, 2, 0)
+
+    def second_both(i):
+        for h in range(2):
+            ring(i, 0, h, i, 1 + h, 2 + h, along_second(1 + 2 * h))
+        for h in range(2):
+            ring(i, 0, 1 - h, i, 1 + h, 2 + h, along_second(1 + 2 * h))
 
     def product(*slots):
         def step(t, carry):
@@ -151,8 +145,13 @@
 
         lax.fori_loop(0, ROWS // BLOCK, step, 0)
 
+    def step_of(i):
+        if isinstance(i, int):
+            return STEP[i]
+        return jnp.where(i == 0, 0, jnp.where(i == 1, 3, i - 1))
+
     def place(i, j):
-        di, dj = STEP[i], STEP[j]
+        di, dj = step_of(i), step_of(j)
         return (x + di * on_x + dj * on_z) % 4, (z + di * on_z + dj * on_x) % 4
 
     HALF = ROWS // 2
@@ -211,50 +210,59 @@
 
     waiting = []
 
-    def run(*slots):
+    def run(*slots, lag=2):
         product(*slots)
         for i, j in slots:
             pass_on(i, j)
-        for i, j in waiting:
-            add_on(i, j)
-        waiting[:] = slots
+        waiting.append(slots)
+        settle(lag)
+
+    def settle(lag):
+        while len(waiting) > lag:
+            for i, j in waiting.pop(0):
+                add_on(i, j)
+
+    rel = (y - x + 4) % 4
+
+    def pick(other, *by_rel):
+        i = jnp.where(rel == 0, by_rel[0], jnp.where(rel == 1, by_rel[1], jnp.where(rel == 2, by_rel[2], by_rel[3])))
+        return jnp.where(c == 1, other, i)
+
+    order = [pick(0, 1, 1, 0, 2), pick(1, 3, 0, 1, 0), pick(2, 2, 3, 2, 3), pick(3, 0, 2, 3, 1)]
+
+    def neighbours(p):
+        for h in range(2):
+            second_forward(order[p], h)
+        second_rest(order[p])
+        run((order[p], 1), (order[p], 2))
+
+    def across(p, lag=2):
+        for h in range(2):
+            got(order[p], 3, h)
+        run((order[p], 3), lag=lag)
 
     arrived(a_buf.at[1 - c], pair_r.at[1])
     run((0, 0))
-    first_forward()
-    for h in range(2):
-        second_out(1, h)
-    second_forward(0)
-    for h in range(2):
-        second_out(2, h)
+    for h in (c, 1 - c):
+        first_forward(h)
+        got(2 - h, 0, h)
+    second_both(order[0])
     run((1, 0), (2, 0))
-    second_rest(0)
-    run((0, 1), (0, 2))
     got(3, 0, 0)
     got(3, 0, 1)
-    for h in range(2):
-        second_out(3, h)
-    got(0, 3, 0)
-    got(0, 3, 1)
-    second_forward(1)
-    run((3, 0), (0, 3))
-    second_rest(1)
-    run((1, 1), (1, 2))
-    second_forward(2)
-    second_rest(2)
-    run((2, 1), (2, 2))
-    second_forward(3)
-    for i in (1, 2):
-        got(i, 3, 0)
-        got(i, 3, 1)
-    run((1, 3), (2, 3))
-    second_rest(3)
-    run((3, 1), (3, 2))
-    got(3, 3, 0)
-    got(3, 3, 1)
-    run((3, 3))
-    for i, j in waiting:
-        add_on(i, j)
+    second_both(order[1])
+    run((3, 0))
+    neighbours(0)
+    second_both(order[2])
+    neighbours(1)
+    across(0)
+    second_both(order[3])
+    neighbours(2)
+    across(1)
+    neighbours(3)
+    across(2, lag=1)
+    across(3, lag=1)
+    settle(0)
 
     ahead = (y - x + 4) % 4
     slot = (ahead == 1) * 2 + (ahead == 2) * 3 + (ahead == 3) * 1
@@ -363,7 +371,7 @@
         compiler_params=pltpu.CompilerParams(
             collective_id=0, has_side_effects=True, vmem_limit_bytes=60 << 20
         ),
-    )(amplitudes, integrals, amp_mask, int_mask)
+    )(amplitudes, integrals, amp_mask, int_mask.T)
 
 
 def solution(mesh):

time: 144 us -> 124 us (0.86)
  Pallas kernels: 140 us -> 122 us
    pallas_call x1, Pallas kernels: 140 us -> 122 us  [per_device(): pl.pallas_call(kernel, out_shape=jax.ShapeDtypeStruct((ROWS, 4 * WIDE), b...]
    unnamed x2 -> x1, local copies, waits for them, and re-layouts: 3.61 us -> 2.26 us
where the time goes in v2:
time: 124 us
  Pallas kernels  122 us (98%)
  local copies, waits for them, and re-layouts  2.26 us (2%)
    pallas_call x1, Pallas kernels, per_device(): pl.pallas_call(kernel, out_shape=jax.ShapeDtypeStruct((ROWS, 4 * WIDE), b...  122 us

profile of v2, /device:TPU:5, one launch (start us, length us, event | category | flops | bytes accessed | tf_op | source)
XLA Modules:
  0.0 123.9 jit_solution(3192015661224033555)
XLA Ops:
  0.0 121.6 %shard_map.46 = bf16[1024,512]{1,0:T(8,128)(2,1)} custom-call(bf16[1024,2048]{1,0:T(8,128)(2,1)} %a_hbm.1, bf16[2048,256]{1,0:T(8,128)(2,1)} %b_hbm.1, s32[8,16]{1,0:T(8,128)} %am.1, s32[2,16]{1,0:T(2,128)} %bitcast.1), custom_call_target="tpu_custom_call" | custom-call | tf_op jit(solution)/shard_map/pallas_call | solution.py:340
  121.6 2.3 %copy.6 = bf16[1024,512]{1,0:T(8,128)(2,1)} copy(bf16[1024,512]{1,0:T(8,128)(2,1)} %shard_map.46) | data formatting | bytes 2097152

commit v3 on v2

--- a/solution.py
+++ b/solution.py
@@ -11,12 +11,15 @@
 DEPTH = 2048
 WIDE = 128
 BLOCK = 256
+HALF = ROWS // 2
+EXTRA = 16
+STEPS = 256.0
 STEP = (0, 3, 1, 2)
 
 
 def kernel(
     a_hbm, b_hbm, am, im, o_hbm,
-    a_buf, b_raw, b_out, b_buf, c_buf, near, mine, out_buf, out_send,
+    a_buf, b_raw, b_out, b_buf, c_buf, code, near, mine, out_buf, out_send,
     load_sem, pair_s, pair_r, ring_s, ring_r, y_s, y_r, o_s, o_r, store_sem,
 ):
     r, q = lax.axis_index("row"), lax.axis_index("col")
@@ -154,14 +157,33 @@
         di, dj = step_of(i), step_of(j)
         return (x + di * on_x + dj * on_z) % 4, (z + di * on_z + dj * on_x) % 4
 
-    HALF = ROWS // 2
-
     def half(n):
         return pl.ds(n * HALF, HALF)
 
+    def pack(u, n):
+        blocks = [pl.ds(t * TILE, TILE) for t in range(HALF // TILE)]
+        top = jnp.full((1, WIDE), 1e-30, jnp.float32)
+        for rows in blocks:
+            top = jnp.maximum(top, jnp.max(jnp.abs(c_buf.at[u, half(n)][rows, :]), axis=0, keepdims=True))
+        level = jnp.floor(STEPS * jnp.log2(32000.0 / top))
+        scale = jnp.exp2(level / STEPS)
+        for rows in blocks:
+            value = jnp.floor(c_buf.at[u, half(n)][rows, :] * scale + 0.5)
+            code[u, n, rows, :] = value.astype(jnp.int32).astype(jnp.int16)
+        code[u, n, pl.ds(HALF, EXTRA), :] = (
+            jnp.broadcast_to(level, (EXTRA, WIDE)).astype(jnp.int32).astype(jnp.int16)
+        )
+
+    def size_of(ref):
+        level = ref[pl.ds(HALF, EXTRA), :].astype(jnp.int32).astype(jnp.float32)
+        return jnp.exp2(-level[:1, :] / STEPS)
+
+    def decode(ref, rows, size):
+        return ref[rows, :].astype(jnp.int32).astype(jnp.float32) * size
+
     def y_copy(u, n, dst, ss, rs, to):
         return pltpu.make_async_remote_copy(
-            src_ref=c_buf.at[u, half(n)], dst_ref=dst, send_sem=ss, recv_sem=rs, device_id=to, device_id_type=MESH
+            src_ref=code.at[u, n], dst_ref=dst, send_sem=ss, recv_sem=rs, device_id=to, device_id_type=MESH
         )
 
     def far_copy(u, n, zz):
@@ -169,7 +191,7 @@
 
     def near_copy(u, n, side, zz):
         return y_copy(
-            u, n, mine.at[side, zz, half(n)], y_s.at[u, n], y_r.at[2 + side * 2 + n, zz], along_y(3 if side == 0 else 1)
+            u, n, mine.at[side, zz, n], y_s.at[u, n], y_r.at[2 + side * 2 + n, zz], along_y(3 if side == 0 else 1)
         )
 
     def pass_on(i, j):
@@ -179,15 +201,18 @@
 
         @pl.when(role == 2)
         def _():
-            far_copy(u, 0, zz).start()
-            far_copy(u, 1, zz).start()
+            for n in range(2):
+                pack(u, n)
+                far_copy(u, n, zz).start()
 
         @pl.when(role == 1)
         def _():
+            pack(u, 1)
             near_copy(u, 1, 0, zz).start()
 
         @pl.when(role == 3)
         def _():
+            pack(u, 0)
             near_copy(u, 0, 1, zz).start()
 
     def add_on(i, j):
@@ -196,8 +221,13 @@
         role = (y - xx + 4) % 4
 
         def add(n, side):
-            arrived(near.at[n, zz], y_r.at[n, zz])
-            c_buf[u, half(n), :] = c_buf[u, half(n), :] + near[n, zz]
+            ref = near.at[n, zz]
+            arrived(ref, y_r.at[n, zz])
+            size = size_of(ref)
+            for t in range(HALF // TILE):
+                rows = pl.ds(t * TILE, TILE)
+                c_buf.at[u, half(n)][rows, :] = c_buf.at[u, half(n)][rows, :] + decode(ref, rows, size)
+            pack(u, n)
             near_copy(u, n, side, zz).start()
 
         @pl.when(role == 1)
@@ -279,33 +309,34 @@
 
     for j in range(4):
         u, zz = own(j)
-        for side in range(2):
-            for n in range(2):
-                arrived(mine.at[side, zz, half(n)], y_r.at[2 + side * 2 + n, zz])
         spot = (zz % 2) * 2 + c
         stays = zz // 2 == c
 
-        def value(t):
-            rows = pl.ds(pl.multiple_of(t * TILE, TILE), TILE)
-            return rows, (c_buf[u, rows, :] + (mine[0, zz, rows, :] + mine[1, zz, rows, :])).astype(jnp.bfloat16)
+        def finish(put):
+            for n in range(2):
+                refs = [mine.at[side, zz, n] for side in range(2)]
+                for side in range(2):
+                    arrived(refs[side], y_r.at[2 + side * 2 + n, zz])
+                sizes = [size_of(ref) for ref in refs]
+                for t in range(HALF // TILE):
+                    rows = pl.ds(t * TILE, TILE)
+                    others = [decode(ref, rows, size) for ref, size in zip(refs, sizes)]
+                    value = c_buf.at[u, half(n)][rows, :] + (others[0] + others[1])
+                    put(pl.ds(n * HALF + t * TILE, TILE), value.astype(jnp.bfloat16))
 
         @pl.when(stays)
         def _():
-            def step(t, carry):
-                rows, v = value(t)
-                out_buf[spot, rows, :] = v
-                return carry
-
-            lax.fori_loop(0, ROWS // TILE, step, 0)
+            def put(rows, value):
+                out_buf[spot, rows, :] = value
+
+            finish(put)
 
         @pl.when(jnp.logical_not(stays))
         def _():
-            def step(t, carry):
-                rows, v = value(t)
-                out_send[zz % 2, rows, :] = v
-                return carry
-
-            lax.fori_loop(0, ROWS // TILE, step, 0)
+            def put(rows, value):
+                out_send[zz % 2, rows, :] = value
+
+            finish(put)
             send(out_send.at[zz % 2], out_buf.at[spot], o_s.at[zz % 2], o_r.at[zz % 2], sibling)
 
     for n in range(2):
@@ -353,8 +384,9 @@
             pltpu.VMEM((DEPTH, WIDE), bf16),
             pltpu.VMEM((4, 4, 2, DEPTH, WIDE), bf16),
             pltpu.VMEM((16, ROWS, WIDE), f32),
-            pltpu.VMEM((2, 4, ROWS // 2, WIDE), f32),
-            pltpu.VMEM((2, 4, ROWS, WIDE), f32),
+            pltpu.VMEM((16, 2, HALF + EXTRA, WIDE), jnp.int16),
+            pltpu.VMEM((2, 4, HALF + EXTRA, WIDE), jnp.int16),
+            pltpu.VMEM((2, 4, 2, HALF + EXTRA, WIDE), jnp.int16),
             pltpu.VMEM((4, ROWS, WIDE), bf16),
             pltpu.VMEM((2, ROWS, WIDE), bf16),
             dma((3,)),

time: 124 us -> 112 us (0.903)
  Pallas kernels: 122 us -> 109 us
    pallas_call x1, Pallas kernels: 122 us -> 109 us  [per_device(): pl.pallas_call(kernel, out_shape=jax.ShapeDtypeStruct((ROWS, 4 * WIDE), b...]
where the time goes in v3:
time: 112 us; the launch traced here: 111 us
  Pallas kernels  109 us (97%)
  local copies, waits for them, and re-layouts  2.26 us (2%)
    pallas_call x1, Pallas kernels, per_device(): pl.pallas_call(kernel, out_shape=jax.ShapeDtypeStruct((ROWS, 4 * WIDE), b...  109 us
    unnamed x1, local copies, waits for them, and re-layouts  2.26 us

profile of v3, /device:TPU:5, one launch (start us, length us, event | category | flops | bytes accessed | tf_op | source)
XLA Modules:
  0.0 111.5 jit_solution(1178256918611108255)
XLA Ops:
  0.0 109.2 %shard_map.46 = bf16[1024,512]{1,0:T(8,128)(2,1)} custom-call(bf16[1024,2048]{1,0:T(8,128)(2,1)} %a_hbm.1, bf16[2048,256]{1,0:T(8,128)(2,1)} %b_hbm.1, s32[8,16]{1,0:T(8,128)} %am.1, s32[2,16]{1,0:T(2,128)} %bitcast.1), custom_call_target="tpu_custom_call" | custom-call | tf_op jit(solution)/shard_map/pallas_call | solution.py:371
  109.2 2.3 %copy.6 = bf16[1024,512]{1,0:T(8,128)(2,1)} copy(bf16[1024,512]{1,0:T(8,128)(2,1)} %shard_map.46) | data formatting | bytes 2097152

commit v4 on v3

--- a/solution.py
+++ b/solution.py
@@ -18,9 +18,9 @@
 
 
 def kernel(
-    a_hbm, b_hbm, am, im, o_hbm,
-    a_buf, b_raw, b_out, b_buf, c_buf, code, near, mine, out_buf, out_send,
-    load_sem, pair_s, pair_r, ring_s, ring_r, y_s, y_r, o_s, o_r, store_sem,
+    a_hbm, b_hbm, am, im, o_ref,
+    a_buf, b_raw, b_out, b_buf, c_buf, code, near, mine, out_send,
+    load_sem, pair_s, pair_r, ring_s, ring_r, y_s, y_r, o_s, o_r,
 ):
     r, q = lax.axis_index("row"), lax.axis_index("col")
     x, z, y, c = r // 4, r % 4, q // 2, q % 2
@@ -133,7 +133,7 @@
         for h in range(2):
             ring(i, 0, 1 - h, i, 1 + h, 2 + h, along_second(1 + 2 * h))
 
-    def product(*slots):
+    def product(*slots, first=0, last=ROWS // BLOCK):
         def step(t, carry):
             rows = pl.ds(pl.multiple_of(t * BLOCK, BLOCK), BLOCK)
             total = None
@@ -146,7 +146,7 @@
                 c_buf[i * 4 + j, rows, :] = total[:, n * WIDE : (n + 1) * WIDE]
             return carry
 
-        lax.fori_loop(0, ROWS // BLOCK, step, 0)
+        lax.fori_loop(first, last, step, 0)
 
     def step_of(i):
         if isinstance(i, int):
@@ -194,26 +194,20 @@
             u, n, mine.at[side, zz, n], y_s.at[u, n], y_r.at[2 + side * 2 + n, zz], along_y(3 if side == 0 else 1)
         )
 
-    def pass_on(i, j):
+    def pass_on(i, j, n):
         u = i * 4 + j
         xx, zz = place(i, j)
         role = (y - xx + 4) % 4
 
         @pl.when(role == 2)
         def _():
-            for n in range(2):
-                pack(u, n)
-                far_copy(u, n, zz).start()
-
-        @pl.when(role == 1)
-        def _():
-            pack(u, 1)
-            near_copy(u, 1, 0, zz).start()
-
-        @pl.when(role == 3)
-        def _():
-            pack(u, 0)
-            near_copy(u, 0, 1, zz).start()
+            pack(u, n)
+            far_copy(u, n, zz).start()
+
+        @pl.when(role == (1 if n == 1 else 3))
+        def _():
+            pack(u, n)
+            near_copy(u, n, 1 - n, zz).start()
 
     def add_on(i, j):
         u = i * 4 + j
@@ -243,7 +237,8 @@
     def run(*slots, lag=2):
         product(*slots)
         for i, j in slots:
-            pass_on(i, j)
+            for n in range(2):
+                pass_on(i, j, n)
         waiting.append(slots)
         settle(lag)
 
@@ -270,6 +265,39 @@
         for h in range(2):
             got(order[p], 3, h)
         run((order[p], 3), lag=lag)
+
+    ahead = (y - x + 4) % 4
+    slot = (ahead == 1) * 2 + (ahead == 2) * 3 + (ahead == 3) * 1
+
+    def out_at(spot):
+        return o_ref.at[:, pl.ds(pl.multiple_of(spot * WIDE, WIDE), WIDE)]
+
+    def finish(p):
+        u = jnp.where(c == 0, slot * 4 + p, p * 4 + slot)
+        zz = (z + STEP[p]) % 4
+        spot = (zz % 2) * 2 + c
+        stays = zz // 2 == c
+
+        def total(ref):
+            for n in range(2):
+                refs = [mine.at[side, zz, n] for side in range(2)]
+                for side in range(2):
+                    arrived(refs[side], y_r.at[2 + side * 2 + n, zz])
+                sizes = [size_of(r) for r in refs]
+                for t in range(HALF // TILE):
+                    rows = pl.ds(t * TILE, TILE)
+                    others = [decode(r, rows, size) for r, size in zip(refs, sizes)]
+                    value = c_buf.at[u, half(n)][rows, :] + (others[0] + others[1])
+                    ref[pl.ds(n * HALF + t * TILE, TILE), :] = value.astype(jnp.bfloat16)
+
+        @pl.when(stays)
+        def _():
+            total(out_at(spot))
+
+        @pl.when(jnp.logical_not(stays))
+        def _():
+            total(out_send.at[zz % 2])
+            send(out_send.at[zz % 2], out_at(spot), o_s.at[zz % 2], o_r.at[zz % 2], sibling)
 
     arrived(a_buf.at[1 - c], pair_r.at[1])
     run((0, 0))
@@ -290,59 +318,18 @@
     neighbours(2)
     across(1)
     neighbours(3)
-    across(2, lag=1)
-    across(3, lag=1)
-    settle(0)
-
-    ahead = (y - x + 4) % 4
-    slot = (ahead == 1) * 2 + (ahead == 2) * 3 + (ahead == 3) * 1
-
-    def own(j):
-        u = jnp.where(c == 0, slot * 4 + j, j * 4 + slot)
-        zz = (z + STEP[j]) % 4
-        return u, zz
-
-    def store(n):
-        return pltpu.make_async_copy(
-            out_buf.at[n], o_hbm.at[:, pl.ds(n * WIDE, WIDE)], store_sem.at[n]
-        )
-
-    for j in range(4):
-        u, zz = own(j)
-        spot = (zz % 2) * 2 + c
-        stays = zz // 2 == c
-
-        def finish(put):
-            for n in range(2):
-                refs = [mine.at[side, zz, n] for side in range(2)]
-                for side in range(2):
-                    arrived(refs[side], y_r.at[2 + side * 2 + n, zz])
-                sizes = [size_of(ref) for ref in refs]
-                for t in range(HALF // TILE):
-                    rows = pl.ds(t * TILE, TILE)
-                    others = [decode(ref, rows, size) for ref, size in zip(refs, sizes)]
-                    value = c_buf.at[u, half(n)][rows, :] + (others[0] + others[1])
-                    put(pl.ds(n * HALF + t * TILE, TILE), value.astype(jnp.bfloat16))
-
-        @pl.when(stays)
-        def _():
-            def put(rows, value):
-                out_buf[spot, rows, :] = value
-
-            finish(put)
-
-        @pl.when(jnp.logical_not(stays))
-        def _():
-            def put(rows, value):
-                out_send[zz % 2, rows, :] = value
-
-            finish(put)
-            send(out_send.at[zz % 2], out_buf.at[spot], o_s.at[zz % 2], o_r.at[zz % 2], sibling)
-
+    across(2, lag=0)
+    for j in range(3):
+        finish(j)
+    for h in range(2):
+        got(order[3], 3, h)
     for n in range(2):
-        arrived(out_buf.at[n * 2 + 1 - c], o_r.at[n])
-    for n in range(4):
-        store(n).start()
+        product((order[3], 3), first=2 * n, last=2 * n + 2)
+        pass_on(order[3], 3, n)
+    add_on(order[3], 3)
+    finish(3)
+    for n in range(2):
+        arrived(out_at(n * 2 + 1 - c), o_r.at[n])
 
     for copy in started:
         copy.wait_send()
@@ -361,8 +348,6 @@
             src_ref=out_send.at[n], dst_ref=out_send.at[n], send_sem=o_s.at[n], recv_sem=o_s.at[n],
             device_id=sibling, device_id_type=MESH,
         ).wait_send()
-    for n in range(4):
-        store(n).wait()
 
 
 def per_device(amplitudes, integrals, amp_mask, int_mask):
@@ -377,7 +362,7 @@
             pl.BlockSpec(memory_space=pltpu.SMEM),
             pl.BlockSpec(memory_space=pltpu.SMEM),
         ],
-        out_specs=pl.BlockSpec(memory_space=pl.ANY),
+        out_specs=pl.BlockSpec(memory_space=pltpu.VMEM),
         scratch_shapes=[
             pltpu.VMEM((2, ROWS, DEPTH), bf16),
             pltpu.VMEM((2, DEPTH, WIDE), bf16),
@@ -387,7 +372,6 @@
             pltpu.VMEM((16, 2, HALF + EXTRA, WIDE), jnp.int16),
             pltpu.VMEM((2, 4, HALF + EXTRA, WIDE), jnp.int16),
             pltpu.VMEM((2, 4, 2, HALF + EXTRA, WIDE), jnp.int16),
-            pltpu.VMEM((4, ROWS, WIDE), bf16),
             pltpu.VMEM((2, ROWS, WIDE), bf16),
             dma((3,)),
             dma((2,)),
@@ -398,10 +382,9 @@
             dma((6, 4)),
             dma((2,)),
             dma((2,)),
-            dma((4,)),
         ],
         compiler_params=pltpu.CompilerParams(
-            collective_id=0, has_side_effects=True, vmem_limit_bytes=60 << 20
+            collective_id=0, has_side_effects=True, vmem_limit_bytes=52 << 20
         ),
     )(amplitudes, integrals, amp_mask, int_mask.T)
 

time: 112 us -> 110 us (0.982)
  Pallas kernels: 109 us -> 107 us
    pallas_call x1, Pallas kernels: 109 us -> 107 us  [per_device(): pl.pallas_call(kernel, out_shape=jax.ShapeDtypeStruct((ROWS, 4 * WIDE), b...]
    unnamed x1 -> x5, local copies, waits for them, and re-layouts: 2.26 us -> 2.34 us
where the time goes in v4:
time: 110 us
  Pallas kernels  107 us (97%)
  local copies, waits for them, and re-layouts  2.34 us (2%)
    pallas_call x1, Pallas kernels, per_device(): pl.pallas_call(kernel, out_shape=jax.ShapeDtypeStruct((ROWS, 4 * WIDE), b...  107 us
    unnamed x5, local copies, waits for them, and re-layouts  2.34 us

profile of v4, /device:TPU:5, one launch (start us, length us, event | category | flops | bytes accessed | tf_op | source)
XLA Modules:
  0.0 109.5 jit_solution(12308655758629651491)
XLA Ops:
  0.0 0.0 copy-start
  0.0 0.7 copy-done
  0.7 0.0 copy-start.1
  0.7 0.7 copy-done.1
  1.4 107.2 %shard_map.46 = bf16[1024,512]{1,0:T(8,128)(2,1)S(1)} custom-call(bf16[1024,2048]{1,0:T(8,128)(2,1)} %a_hbm.1, bf16[2048,256]{1,0:T(8,128)(2,1)} %b_hbm.1, s32[8,16]{1,0:T(8,128)S(1)} %copy-done, s32[2,16]{1,0:T(2,128)S(1)} %bitcast.1), custom_call_target="tpu_custom_call" | custom-call | tf_op jit(solution)/shard_map/pallas_call | solution.py:356
  108.5 1.0 copy.6
Async XLA Ops:
  0.0 0.7 copy-start
  0.7 0.7 copy-start.1

commit v5 on v4

--- a/solution.py
+++ b/solution.py
@@ -126,6 +126,10 @@
     def second_rest(i):
         got(i, 1, 1)
         got(i, 2, 0)
+
+    def second_out(i, h):
+        ring(i, 0, h, i, 1, 2, along_second(1))
+        ring(i, 0, h, i, 2, 3, along_second(3))
 
     def second_both(i):
         for h in range(2):
@@ -304,7 +308,7 @@
     for h in (c, 1 - c):
         first_forward(h)
         got(2 - h, 0, h)
-    second_both(order[0])
+        second_out(order[0], h)
     run((1, 0), (2, 0))
     got(3, 0, 0)
     got(3, 0, 1)

time: 110 us -> 108 us (0.982)
    pallas_call x1, Pallas kernels: 107 us -> 106 us  [per_device(): pl.pallas_call(kernel, out_shape=jax.ShapeDtypeStruct((ROWS, 4 * WIDE), b...]
where the time goes in v5:
time: 108 us
  Pallas kernels  106 us (98%)
  local copies, waits for them, and re-layouts  2.34 us (2%)
    pallas_call x1, Pallas kernels, per_device(): pl.pallas_call(kernel, out_shape=jax.ShapeDtypeStruct((ROWS, 4 * WIDE), b...  106 us
    unnamed x5, local copies, waits for them, and re-layouts  2.34 us

profile of v5, /device:TPU:5, one launch (start us, length us, event | category | flops | bytes accessed | tf_op | source)
XLA Modules:
  0.0 108.2 jit_solution(4437764981767870203)
XLA Ops:
  0.0 0.0 copy-start
  0.0 0.7 copy-done
  0.7 0.0 copy-start.1
  0.7 0.7 copy-done.1
  1.4 105.9 %shard_map.46 = bf16[1024,512]{1,0:T(8,128)(2,1)S(1)} custom-call(bf16[1024,2048]{1,0:T(8,128)(2,1)} %a_hbm.1, bf16[2048,256]{1,0:T(8,128)(2,1)} %b_hbm.1, s32[8,16]{1,0:T(8,128)S(1)} %copy-done, s32[2,16]{1,0:T(2,128)S(1)} %bitcast.1), custom_call_target="tpu_custom_call" | custom-call | tf_op jit(solution)/shard_map/pallas_call | solution.py:360
  107.3 1.0 copy.6
Async XLA Ops:
  0.0 0.7 copy-start
  0.7 0.7 copy-start.1

commit v6 on v5

--- a/solution.py
+++ b/solution.py
@@ -18,8 +18,8 @@
 
 
 def kernel(
-    a_hbm, b_hbm, am, im, o_ref,
-    a_buf, b_raw, b_out, b_buf, c_buf, code, near, mine, out_send,
+    a_hbm, b_hbm, am_hbm, im_hbm, o_ref,
+    a_buf, b_raw, b_out, b_buf, c_buf, code, near, mine, out_send, am, im,
     load_sem, pair_s, pair_r, ring_s, ring_r, y_s, y_r, o_s, o_r,
 ):
     r, q = lax.axis_index("row"), lax.axis_index("col")
@@ -58,6 +58,12 @@
         pltpu.make_async_copy(b_hbm.at[:, pl.ds(h * WIDE, WIDE)], b_raw.at[h], load_sem.at[h])
         for h in range(2)
     ] + [pltpu.make_async_copy(a_hbm, a_buf.at[c], load_sem.at[2])]
+    masks = [
+        pltpu.make_async_copy(im_hbm, im, load_sem.at[3]),
+        pltpu.make_async_copy(am_hbm, am, load_sem.at[4]),
+    ]
+    for mask in masks:
+        mask.start()
     for load in loads:
         load.start()
 
@@ -70,6 +76,7 @@
 
     loads[0].wait()
     loads[1].wait()
+    masks[0].wait()
 
     def mask_b(t, carry):
         rows = pl.ds(pl.multiple_of(t * TILE, TILE), TILE)
@@ -101,6 +108,7 @@
     first_out(c)
 
     loads[2].wait()
+    masks[1].wait()
 
     def mask_a(t, carry):
         rows = pl.ds(pl.multiple_of(t * TILE, TILE), TILE)
@@ -363,8 +371,8 @@
         in_specs=[
             pl.BlockSpec(memory_space=pl.ANY),
             pl.BlockSpec(memory_space=pl.ANY),
-            pl.BlockSpec(memory_space=pltpu.SMEM),
-            pl.BlockSpec(memory_space=pltpu.SMEM),
+            pl.BlockSpec(memory_space=pltpu.HBM),
+            pl.BlockSpec(memory_space=pltpu.HBM),
         ],
         out_specs=pl.BlockSpec(memory_space=pltpu.VMEM),
         scratch_shapes=[
@@ -377,7 +385,9 @@
             pltpu.VMEM((2, 4, HALF + EXTRA, WIDE), jnp.int16),
             pltpu.VMEM((2, 4, 2, HALF + EXTRA, WIDE), jnp.int16),
             pltpu.VMEM((2, ROWS, WIDE), bf16),
-            dma((3,)),
+            pltpu.SMEM((8, 16), jnp.int32),
+            pltpu.SMEM((2, 16), jnp.int32),
+            dma((5,)),
             dma((2,)),
             dma((2,)),
             dma((4, 4, 2, 4)),
@@ -390,7 +400,7 @@
         compiler_params=pltpu.CompilerParams(
             collective_id=0, has_side_effects=True, vmem_limit_bytes=52 << 20
         ),
-    )(amplitudes, integrals, amp_mask, int_mask.T)
+    )(amplitudes, integrals, pltpu.with_memory_space_constraint(amp_mask, pltpu.HBM), pltpu.with_memory_space_constraint(int_mask.T, pltpu.HBM))
 
 
 def solution(mesh):

time: 108 us -> 106 us (0.981)
  local copies, waits for them, and re-layouts: 2.34 us -> 0.97 us
    unnamed x5 -> x1, local copies, waits for them, and re-layouts: 2.34 us -> 0.97 us
where the time goes in v6:
time: 106 us
  Pallas kernels  105 us (99%)
    pallas_call x1, Pallas kernels, per_device(): pl.pallas_call(kernel, out_shape=jax.ShapeDtypeStruct((ROWS, 4 * WIDE), b...  105 us

profile of v6, /device:TPU:5, one launch (start us, length us, event | category | flops | bytes accessed | tf_op | source)
XLA Modules:
  0.0 106.2 jit_solution(8183065744020557725)
XLA Ops:
  0.0 105.2 %shard_map.46 = bf16[1024,512]{1,0:T(8,128)(2,1)S(1)} custom-call(bf16[1024,2048]{1,0:T(8,128)(2,1)} %a_hbm.1, bf16[2048,256]{1,0:T(8,128)(2,1)} %b_hbm.1, s32[8,16]{1,0:T(8,128)} %am_hbm.1, s32[2,16]{1,0:T(2,128)} %bitcast.1), custom_call_target="tpu_custom_call" | custom-call | tf_op jit(solution)/shard_map/pallas_call | solution.py:368
  105.2 1.0 copy.6
